TPU v7x, 256 devices: a whole 4x4x8 slice. The times are simulated.
256 devices in a mesh: tok: 32 (over x, y, core), feat: 8 (over z).
Axes of the slice: x: 4, y: 4, z: 8, core: 2. Of those that a mesh axis runs over, the one named last changes fastest.
Arguments:
- inputs: bfloat16 [16384, 2048], P(('tok', 'feat'))
- norm_gain: float32 [2048], replicated, may hold values from 0.1 to 1.9
- w_in: bfloat16 [512, 8192], P('tok', 'feat'), may hold values from -0.25 to 0.25
- w_out: bfloat16 [512, 8192], P('tok', 'feat'), may hold values from -0.125 to 0.125
- block_index: int32 [64, 4], P('feat'), may hold values from 0 to 15, all different within a row
- segment_ids: int32 [16384], P(('tok', 'feat')), may hold values from 0 to 1023, never falling along the last dimension, each value on 1 to 24 neighbouring positions
- teacher_scores: float32 [1024], replicated, may hold values from -6 to 6
- upstream: bfloat16 [16384, 2048], P(('tok', 'feat')), may hold values from -6 to 6
- readout: float32 [2048], replicated, may hold values from -0.125 to 0.125
Outputs:
- layer_out: bfloat16 [16384, 2048], P(('tok', 'feat'))
- input_grad: bfloat16 [16384, 2048], P(('tok', 'feat'))
- grad_in: float32 [512, 8192], P('tok', 'feat')
- grad_out: float32 [512, 8192], P('tok', 'feat')
Inputs may be any that keep to these rules, and one draw needn't show every extreme that they name: `block_index`: each row names 4 different feature blocks; every feature block is named by some row. `segment_ids`: never falls along the tokens; every segment 0 to 1023 holds 1 to 24 tokens.
All inputs are finite; a program needn't handle non-finite values.
Results may differ from a plain program's by a relative error of at most 0.015.
Values may be sent and summed in bfloat16 or wider, within the bound.
A program may use at most 128 MiB of HBM per device.

v0:
```python
import math
import jax
import jax.numpy as jnp
from jax import lax
from jax.sharding import PartitionSpec as P

BLK = 128
EPS = 1e-06
LOSS_WEIGHT = 8.0


def gelu_tanh(values):
    return jax.nn.gelu(values, approximate=True)


def gelu_back(values, cotangent):
    return jax.vjp(gelu_tanh, values)[1](cotangent)[0]


def on_device(
    inputs, norm_gain, w_in, w_out, block_index, segment_ids, teacher_scores, upstream, readout
):
    local_tokens, model_width = inputs.shape
    blocks_here = w_in.shape[1] // BLK
    feature_blocks = model_width // BLK
    per_hidden = block_index.shape[1]
    total_tokens = local_tokens * lax.axis_size("tok") * lax.axis_size("feat")
    grad_scale = 1.0 / math.sqrt(total_tokens)
    inputs_wide = inputs.astype(jnp.float32)
    mean_square = jnp.mean(inputs_wide * inputs_wide, axis=1, keepdims=True)
    inv_rms = lax.rsqrt(mean_square + EPS)
    normed = (inputs_wide * inv_rms * norm_gain[None, :]).astype(jnp.bfloat16)
    w_in_all, w_out_all = (
        lax.all_gather(w_in, "tok", axis=0, tiled=True),
        lax.all_gather(w_out, "tok", axis=0, tiled=True),
    )
    picked_width = w_in_all.shape[0]
    w_in_blocks = w_in_all.reshape(picked_width, blocks_here, BLK)
    w_out_blocks = w_out_all.reshape(picked_width, blocks_here, BLK)
    normed_rows = lax.all_gather(normed, "feat", axis=0, tiled=True)
    group_rows = normed_rows.shape[0]
    one_hot = block_index[:, :, None] == jnp.arange(feature_blocks, dtype=jnp.int32)[None, None, :]
    sel_half = one_hot.astype(jnp.bfloat16)
    sel_wide = one_hot.astype(jnp.float32)

    def select(rows):
        blocks = rows.reshape(group_rows, feature_blocks, BLK)
        picked = jnp.einsum("rdc,jkd->rjkc", blocks, sel_half, preferred_element_type=jnp.float32)
        return picked.astype(jnp.bfloat16).reshape(group_rows, blocks_here, picked_width)

    def spread(terms):
        grouped = terms.reshape(group_rows, blocks_here, per_hidden, BLK)
        placed = jnp.einsum("rjkc,jkd->rdc", grouped, sel_wide, precision=lax.Precision.HIGHEST)
        return placed.reshape(group_rows, model_width)

    chosen = select(normed_rows)
    pre_act = jnp.einsum("rjm,mjc->rjc", chosen, w_in_blocks, preferred_element_type=jnp.float32)
    activated = gelu_tanh(pre_act).astype(jnp.bfloat16)
    out_terms_fwd = jnp.einsum(
        "rjc,mjc->rjm", activated, w_out_blocks, preferred_element_type=jnp.float32
    )
    branch = lax.psum_scatter(
        spread(out_terms_fwd).astype(jnp.bfloat16), "feat", scatter_dimension=0, tiled=True
    ).astype(jnp.float32)
    layer_out = (inputs_wide + branch).astype(jnp.bfloat16)
    token_score = jnp.dot(layer_out.astype(jnp.float32), readout, precision=lax.Precision.HIGHEST)
    segment_count = teacher_scores.shape[0]
    member = (segment_ids[:, None] == jnp.arange(segment_count, dtype=jnp.int32)[None, :]).astype(
        jnp.float32
    )
    score_sums = jnp.dot(token_score, member, precision=lax.Precision.HIGHEST)
    token_counts = jnp.sum(member, axis=0)
    score_sums, token_counts = lax.psum((score_sums, token_counts), ("tok", "feat"))
    misfit = score_sums / token_counts - teacher_scores
    token_coeff = 2.0 * LOSS_WEIGHT * jnp.sum(member * misfit[None, :], axis=1)
    cotangent_local = (
        upstream.astype(jnp.float32) + token_coeff[:, None] * readout[None, :]
    ).astype(jnp.bfloat16)
    cotangent_rows = lax.all_gather(cotangent_local, "feat", axis=0, tiled=True)
    chosen_grad = select(cotangent_rows)
    upper_grad = jnp.einsum(
        "rjm,mjc->rjc", chosen_grad, w_out_blocks, preferred_element_type=jnp.float32
    )
    pre_grad = gelu_back(pre_act, upper_grad).astype(jnp.bfloat16)

    def arrange(terms):
        return terms.reshape(picked_width, blocks_here * BLK) * grad_scale

    back_terms = jnp.einsum(
        "rjc,mjc->rjm", pre_grad, w_in_blocks, preferred_element_type=jnp.float32
    )
    out_terms = jnp.einsum(
        "rjm,rjc->mjc", chosen_grad, activated, preferred_element_type=jnp.float32
    )
    in_terms = jnp.einsum("rjm,rjc->mjc", chosen, pre_grad, preferred_element_type=jnp.float32)
    grad_out, grad_in = (
        lax.psum_scatter(
            arrange(out_terms).astype(jnp.bfloat16), "tok", scatter_dimension=0, tiled=True
        ).astype(jnp.float32),
        lax.psum_scatter(
            arrange(in_terms).astype(jnp.bfloat16), "tok", scatter_dimension=0, tiled=True
        ).astype(jnp.float32),
    )
    back_sum = lax.psum_scatter(
        spread(back_terms).astype(jnp.bfloat16), "feat", scatter_dimension=0, tiled=True
    ).astype(jnp.float32)
    scaled = back_sum * norm_gain[None, :]
    inner_mean = jnp.mean(scaled * inputs_wide, axis=1, keepdims=True)
    norm_back = inv_rms * scaled - inputs_wide * (inv_rms * inv_rms * inv_rms) * inner_mean
    input_grad = (cotangent_local.astype(jnp.float32) + norm_back).astype(jnp.bfloat16)
    return (layer_out, input_grad, grad_in, grad_out)


def solution(mesh):
    return jax.shard_map(
        on_device,
        mesh=mesh,
        in_specs=(
            P(("tok", "feat"), None),
            P(),
            P("tok", "feat"),
            P("tok", "feat"),
            P("feat", None),
            P(("tok", "feat")),
            P(),
            P(("tok", "feat"), None),
            P(),
        ),
        out_specs=(
            P(("tok", "feat"), None),
            P(("tok", "feat"), None),
            P("tok", "feat"),
            P("tok", "feat"),
        ),
        check_vma=False,
    )
```

profile of v0, /device:TPU:2, one launch (start us, length us, event | category | flops | bytes accessed | tf_op | source)
XLA Modules:
  0.0 581.6 jit_solution(5638336384249948303)
XLA Ops:
  11.7 49.1 %all-gather.7.cloned.1.call-done = bf16[512,1024]{1,0:T(8,128)(2,1)} async-done(((bf16[16,1024]{1,0:T(8,128)(2,1)}), bf16[512,1024]{1,0:T(8,128)(2,1)}) %all-gather.7.cloned.1.call-update) | async-done | bytes 1048592 | tf_op jit(solution)/shard_map/all_gather | solution.py:34
  62.3 48.1 %all-gather.9.cloned.1.call-done = bf16[512,1024]{1,0:T(8,128)(2,1)} async-done(((bf16[16,1024]{1,0:T(8,128)(2,1)}), bf16[512,1024]{1,0:T(8,128)(2,1)}) %all-gather.9.cloned.1.call-update) | async-done | bytes 1048592 | tf_op jit(solution)/shard_map/all_gather | solution.py:35
  111.8 41.5 %all-gather.5.cloned.1.call-done = bf16[512,2048]{1,0:T(8,128)(2,1)} async-done(((bf16[64,2048]{1,0:T(8,128)(2,1)}), bf16[512,2048]{1,0:T(8,128)(2,1)}) %all-gather.5.cloned.1.call-update) | async-done | bytes 2097168 | tf_op jit(solution)/shard_map/all_gather | solution.py:40
  153.3 2.2 copy.82
  159.5 4.5 fusion.47
  164.1 10.4 %copy.61 = f32[512,8,4,128]{3,1,2,0:T(8,128)} copy(f32[512,8,4,128]{0,3,2,1:T(8,128)} %bitcast.104) | data formatting | bytes 16777216 | tf_op jit(solution)/shard_map/reshape | solution.py:52
  174.5 5.6 bitcast_convert_fusion.1
  180.1 1.9 copy.107
  182.7 40.9 %reduce-scatter.5.cloned.1.call-done = bf16[64,2048]{1,0:T(8,128)(2,1)} async-done(((bf16[512,2048]{1,0:T(8,128)(2,1)}), bf16[64,2048]{1,0:T(8,128)(2,1)}) %reduce-scatter.5.cloned.1.call-update) | async-done | bytes 262160 | tf_op jit(solution)/shard_map/reduce_scatter | solution.py:62
  225.9 74.4 %all-reduce = (f32[1024]{0:T(1024)S(1)}, f32[1024]{0:T(1024)S(1)}) all-reduce(f32[1024]{0:T(1024)S(1)} %bitcast.124, f32[1024]{0:T(1024)S(1)} %convert_reduce_fusion), channel_id=1, replica_groups=mesh['tok'=32,'feat'=8] {'tok','feat'}, use_global_device_ids=true, to_apply=%region_2.0 | all-reduce | flops 2048 | bytes 16384 | tf_op jit(solution)/shard_map/psum | solution.py:73
  301.6 37.5 %all-gather.11.cloned.1.call-done = bf16[512,2048]{1,0:T(8,128)(2,1)} async-done(((bf16[64,2048]{1,0:T(8,128)(2,1)}), bf16[512,2048]{1,0:T(8,128)(2,1)}) %all-gather.11.cloned.1.call-update) | async-done | bytes 2097168 | tf_op jit(solution)/shard_map/all_gather | solution.py:79
  339.1 2.2 copy.84
  344.2 3.7 fusion.14
  347.9 3.6 multiply_convert_fusion.1
  351.5 2.4 copy.69
  354.0 6.2 %multiply_convert_fusion = bf16[8,128,512]{2,1,0:T(8,128)(2,1)} fusion(bf16[512,8,512]{2,1,0:T(8,128)(2,1)} %bitcast.116, f32[8,512,128]{2,1,0:T(8,128)S(1)} %copy-done.6), kind=kOutput, calls=%fused_computation.32 | convolution fusion | flops 542638080 | bytes 7340032 | tf_op jit(solution)/shard_map/rjm,rjc->mjc/dot_general | solution.py:92
  360.2 2.4 copy.72
  362.8 4.5 fusion.49
  367.4 10.5 %copy.66 = f32[512,8,4,128]{3,1,2,0:T(8,128)} copy(f32[512,8,4,128]{0,3,2,1:T(8,128)} %bitcast.103) | data formatting | bytes 16777216 | tf_op jit(solution)/shard_map/reshape | solution.py:52
  377.8 5.6 bitcast_convert_fusion
  385.4 52.5 %reduce-scatter.9.cloned.1.call-done = bf16[16,1024]{1,0:T(8,128)(2,1)} async-done(((bf16[512,1024]{1,0:T(8,128)(2,1)}), bf16[16,1024]{1,0:T(8,128)(2,1)}) %reduce-scatter.9.cloned.1.call-update) | async-done | bytes 32784 | tf_op jit(solution)/shard_map/reduce_scatter | solution.py:100
  439.2 87.3 %reduce-scatter.11.cloned.1.call-done = bf16[16,1024]{1,0:T(8,128)(2,1)} async-done(((bf16[512,1024]{1,0:T(8,128)(2,1)}), bf16[16,1024]{1,0:T(8,128)(2,1)}) %reduce-scatter.11.cloned.1.call-update) | async-done | bytes 32784 | tf_op jit(solution)/shard_map/reduce_scatter | solution.py:97
  527.9 43.7 %reduce-scatter.7.cloned.1.call-done = bf16[64,2048]{1,0:T(8,128)(2,1)} async-done(((bf16[512,2048]{1,0:T(8,128)(2,1)}), bf16[64,2048]{1,0:T(8,128)(2,1)}) %reduce-scatter.7.cloned.1.call-update) | async-done | bytes 262160 | tf_op jit(solution)/shard_map/reduce_scatter | solution.py:104
  572.8 2.0 fusion.32
  (73 shorter events, 24.7 us)
Async XLA Ops:
  7.2 53.6 %all-gather.7.cloned.1.call-start = ((), (), s32[]{:S(2)}) async-start(), calls=%async_computation.5 | async-start | bytes 1081344 | tf_op jit(solution)/shard_map/all_gather | solution.py:34
  7.9 102.4 %all-gather.9.cloned.1.call-start = ((), (), s32[]{:S(2)}) async-start(), calls=%async_computation.6 | async-start | bytes 1081344 | tf_op jit(solution)/shard_map/all_gather | solution.py:35
  8.6 144.7 %all-gather.5.cloned.1.call-start = ((), (), s32[]{:S(2)}) async-start(), calls=%async_computation.4 | async-start | bytes 2359296 | tf_op jit(solution)/shard_map/all_gather | solution.py:40
  11.6 212.0 %reduce-scatter.5.cloned.1.call-start = ((), (), s32[]{:S(2)}) async-start(), calls=%async_computation.7 | async-start | bytes 2359296 | tf_op jit(solution)/shard_map/reduce_scatter | solution.py:62
  153.3 2.2 copy-start.12
  157.6 2.0 copy-start.1
  159.5 4.6 copy-start.4
  182.0 41.6 %copy-start = (bf16[64,2048]{1,0:T(8,128)(2,1)S(1)}, bf16[64,2048]{1,0:T(8,128)(2,1)}, u32[]{:S(2)}) copy-start(bf16[64,2048]{1,0:T(8,128)(2,1)} %param.9) | copy-start | bytes 786436
  182.0 43.4 %copy-start.14 = (f32[2048]{0:T(1024)S(1)}, f32[2048]{0:T(1024)}, u32[]{:S(2)}) copy-start(f32[2048]{0:T(1024)} %param.17) | copy-start | bytes 24580
  182.0 118.3 %copy-start.15 = (f32[1024]{0:T(1024)S(1)}, f32[1024]{0:T(1024)}, u32[]{:S(2)}) copy-start(f32[1024]{0:T(1024)} %param.15) | copy-start | bytes 12292
  182.0 118.5 %copy-start.9 = (bf16[64,2048]{1,0:T(8,128)(2,1)S(1)}, bf16[64,2048]{1,0:T(8,128)(2,1)}, u32[]{:S(2)}) copy-start(bf16[64,2048]{1,0:T(8,128)(2,1)} %param.16) | copy-start | bytes 786436
  182.0 157.0 %all-gather.11.cloned.1.call-start = ((), (), s32[]{:S(2)}) async-start(), calls=%async_computation.8 | async-start | bytes 2359296 | tf_op jit(solution)/shard_map/all_gather | solution.py:79
  224.6 0.7 copy-start.11
  301.4 136.4 %reduce-scatter.9.cloned.1.call-start = ((), (), s32[]{:S(2)}) async-start(), calls=%async_computation.10 | async-start | bytes 1081344 | tf_op jit(solution)/shard_map/reduce_scatter | solution.py:100
  342.6 1.6 copy-start.5
  343.3 4.5 copy-start.3
  344.2 3.7 copy-start.2
  347.9 3.6 copy-start.7
  351.5 2.5 copy-start.6
  353.9 172.6 %reduce-scatter.11.cloned.1.call-start = ((), (), s32[]{:S(2)}) async-start(), calls=%async_computation.11 | async-start | bytes 1081344 | tf_op jit(solution)/shard_map/reduce_scatter | solution.py:97
  360.2 2.7 copy-start.8
  362.6 209.1 %reduce-scatter.7.cloned.1.call-start = ((), (), s32[]{:S(2)}) async-start(), calls=%async_computation.9 | async-start | bytes 2359296 | tf_op jit(solution)/shard_map/reduce_scatter | solution.py:104
  385.3 186.3 %copy-start.13 = (f32[2048]{0:T(1024)S(1)}, f32[2048]{0:T(1024)}, u32[]{:S(2)}) copy-start(f32[2048]{0:T(1024)} %param.10) | copy-start | bytes 24580
  385.4 187.4 %copy-start.10 = (bf16[64,2048]{1,0:T(8,128)(2,1)S(1)}, bf16[64,2048]{1,0:T(8,128)(2,1)}, u32[]{:S(2)}) copy-start(bf16[64,2048]{1,0:T(8,128)(2,1)} %param.16) | copy-start | bytes 786436
  (1 other events, 0.7 us)
Sparse Core Ops, SparseCore 0:
  10.5 50.1 all-gather.6
  63.3 46.9 all-gather.8
  112.7 40.5 all-gather.4
  182.1 41.4 reduce-scatter.4
  301.5 37.5 all-gather.10
  354.1 83.7 reduce-scatter.8
  441.6 84.8 reduce-scatter.10
  529.1 42.5 reduce-scatter.6
where the time goes:
time: 583 us; the launch traced here: 582 us
  waiting for transfers between devices  402 us (69%)
  blocking collectives  74.4 us (13%)
  local copies, waits for them, and re-layouts  41 us (7%)
  matrix products  38.3 us (7%)
  between operations  14.4 us (2%)
  other arithmetic  11 us (2%)
    reduce_scatter x1, waiting for transfers between devices, on_device(): lax.psum_scatter(arrange(out_terms).astype(jnp.bfloat16), 'tok', scatter_...  87.3 us
    psum x1, blocking collectives, on_device(): lax.psum((score_sums, token_counts), ('tok', 'feat'))  74.4 us
    reduce_scatter x1, waiting for transfers between devices, on_device(): lax.psum_scatter(arrange(in_terms).astype(jnp.bfloat16), 'tok', scatter_d...  52.5 us
    all_gather x1, waiting for transfers between devices, on_device(): lax.all_gather(w_in, 'tok', axis=0, tiled=True)  49.1 us
    all_gather x1, waiting for transfers between devices, on_device(): lax.all_gather(w_out, 'tok', axis=0, tiled=True)  48.1 us
    reduce_scatter x1, waiting for transfers between devices, on_device(): lax.psum_scatter(spread(back_terms).astype(jnp.bfloat16), 'feat', scatter...  43.7 us
    all_gather x1, waiting for transfers between devices, on_device(): normed_rows = lax.all_gather(normed, 'feat', axis=0, tiled=True)  41.5 us
    reduce_scatter x1, waiting for transfers between devices, on_device(): lax.psum_scatter(spread(out_terms_fwd).astype(jnp.bfloat16), 'feat', scat...  40.9 us
  transfers between devices with their start and end apart: 8, of which 8 were waited for; matrix products, arithmetic and copies ran while one was open for 7% of the time, Pallas kernels for 0%

commit v1 on v0

--- a/solution.py
+++ b/solution.py
@@ -32,7 +32,9 @@
     normed = (inputs_wide * inv_rms * norm_gain[None, :]).astype(jnp.bfloat16)
     w_in_all, w_out_all = (
         lax.all_gather(w_in, "tok", axis=0, tiled=True),
-        lax.all_gather(w_out, "tok", axis=0, tiled=True),
+        jnp.concatenate(
+            lax.all_to_all(jnp.stack([w_out] * lax.axis_size("tok")), "tok", 0, 0), axis=0
+        ),
     )
     picked_width = w_in_all.shape[0]
     w_in_blocks = w_in_all.reshape(picked_width, blocks_here, BLK)

time: 583 us -> 536 us (0.919)
  waiting for transfers between devices: 402 us -> 334 us
  blocking collectives: 74.4 us -> 96.6 us
    all_gather x1 -> x0, waiting for transfers between devices: 48.1 us -> none  [on_device(): lax.all_gather(w_out, 'tok', axis=0, tiled=True)]
    all_to_all x0 -> x1, blocking collectives: none -> 22.1 us  [on_device(): lax.all_to_all(jnp.stack([w_out] * lax.axis_size('tok')), 'tok', 0, 0)]
    all_gather x1, waiting for transfers between devices: 49.1 us -> 29.7 us  [on_device(): lax.all_gather(w_in, 'tok', axis=0, tiled=True)]
  transfers between devices with their start and end apart: 8 -> 7, of which waited for: 8 -> 7; matrix products, arithmetic and copies ran while one was open for 7% -> 7% of each run, Pallas kernels for 0% -> 0%
where the time goes in v1:
time: 536 us; the launch traced here: 535 us
  waiting for transfers between devices  334 us (62%)
  blocking collectives  96.6 us (18%)
  local copies, waits for them, and re-layouts  40.6 us (8%)
  matrix products  38.4 us (7%)
  between operations  14.4 us (3%)
  other arithmetic  11 us (2%)
    reduce_scatter x1, waiting for transfers between devices, on_device(): lax.psum_scatter(arrange(out_terms).astype(jnp.bfloat16), 'tok', scatter_...  87.2 us
    psum x1, blocking collectives, on_device(): lax.psum((score_sums, token_counts), ('tok', 'feat'))  74.5 us
    reduce_scatter x1, waiting for transfers between devices, on_device(): lax.psum_scatter(arrange(in_terms).astype(jnp.bfloat16), 'tok', scatter_d...  52.5 us
    reduce_scatter x1, waiting for transfers between devices, on_device(): lax.psum_scatter(spread(back_terms).astype(jnp.bfloat16), 'feat', scatter...  43.7 us
    all_gather x1, waiting for transfers between devices, on_device(): normed_rows = lax.all_gather(normed, 'feat', axis=0, tiled=True)  41.5 us
    reduce_scatter x1, waiting for transfers between devices, on_device(): lax.psum_scatter(spread(out_terms_fwd).astype(jnp.bfloat16), 'feat', scat...  40.8 us
    all_gather x1, waiting for transfers between devices, on_device(): cotangent_rows = lax.all_gather(cotangent_local, 'feat', axis=0, tiled=True)  37.5 us
    all_gather x1, waiting for transfers between devices, on_device(): lax.all_gather(w_in, 'tok', axis=0, tiled=True)  29.7 us
  transfers between devices with their start and end apart: 7, of which 7 were waited for; matrix products, arithmetic and copies ran while one was open for 7% of the time, Pallas kernels for 0%

profile of v1, /device:TPU:2, one launch (start us, length us, event | category | flops | bytes accessed | tf_op | source)
XLA Modules:
  0.0 535.2 jit_solution(5882639989818358755)
XLA Ops:
  11.8 22.1 %all_to_all.5 = bf16[32,16,1024]{2,1,0:T(8,128)(2,1)S(1)} all-to-all(bf16[32,16,1024]{2,1,0:T(8,128)(2,1)S(1)} %stack.2), channel_id=1, replica_groups=mesh['tok'=32,'feat'=8] {'tok'}, dimensions={0} | all-to-all | bytes 2097152 | tf_op jit(solution)/shard_map/all_to_all | solution.py:36
  34.1 29.7 %all-gather.6.cloned.1.call-done = bf16[512,1024]{1,0:T(8,128)(2,1)} async-done(((bf16[16,1024]{1,0:T(8,128)(2,1)}), bf16[512,1024]{1,0:T(8,128)(2,1)}) %all-gather.6.cloned.1.call-update) | async-done | bytes 1048592 | tf_op jit(solution)/shard_map/all_gather | solution.py:34
  65.4 41.5 %all-gather.4.cloned.1.call-done = bf16[512,2048]{1,0:T(8,128)(2,1)} async-done(((bf16[64,2048]{1,0:T(8,128)(2,1)}), bf16[512,2048]{1,0:T(8,128)(2,1)}) %all-gather.4.cloned.1.call-update) | async-done | bytes 2097168 | tf_op jit(solution)/shard_map/all_gather | solution.py:42
  106.9 2.2 copy.77
  113.0 4.6 fusion.26
  117.6 10.4 %copy.58 = f32[512,8,4,128]{3,1,2,0:T(8,128)} copy(f32[512,8,4,128]{0,3,2,1:T(8,128)} %bitcast.104) | data formatting | bytes 16777216 | tf_op jit(solution)/shard_map/reshape | solution.py:54
  128.0 5.6 %bitcast_convert_fusion.1 = bf16[16,512,128]{2,0,1:T(8,128)(2,1)S(1)} fusion(f32[512,8,4,128]{3,1,2,0:T(8,128)} %copy.58, s32[8,4]{0,1:T(4,128)S(1)} %copy-done.12), kind=kOutput, calls=%fused_computation.1 | convolution fusion | flops 403702272 | bytes 10485888 | tf_op jit(solution)/shard_map/rjkc,jkd->rdc/dot_general | solution.py:55
  133.6 1.9 copy.107
  136.3 40.8 %reduce-scatter.5.cloned.1.call-done = bf16[64,2048]{1,0:T(8,128)(2,1)} async-done(((bf16[512,2048]{1,0:T(8,128)(2,1)}), bf16[64,2048]{1,0:T(8,128)(2,1)}) %reduce-scatter.5.cloned.1.call-update) | async-done | bytes 262160 | tf_op jit(solution)/shard_map/reduce_scatter | solution.py:64
  179.4 74.5 %all-reduce = (f32[1024]{0:T(1024)S(1)}, f32[1024]{0:T(1024)S(1)}) all-reduce(f32[1024]{0:T(1024)S(1)} %bitcast.125, f32[1024]{0:T(1024)S(1)} %convert_reduce_fusion), channel_id=1, replica_groups=mesh['tok'=32,'feat'=8] {'tok','feat'}, use_global_device_ids=true, to_apply=%region_2.0 | all-reduce | flops 2048 | bytes 16384 | tf_op jit(solution)/shard_map/psum | solution.py:75
  255.2 37.5 %all-gather.8.cloned.1.call-done = bf16[512,2048]{1,0:T(8,128)(2,1)} async-done(((bf16[64,2048]{1,0:T(8,128)(2,1)}), bf16[512,2048]{1,0:T(8,128)(2,1)}) %all-gather.8.cloned.1.call-update) | async-done | bytes 2097168 | tf_op jit(solution)/shard_map/all_gather | solution.py:81
  292.7 2.2 copy.80
  297.8 3.8 fusion.14
  301.6 3.6 multiply_convert_fusion.1
  305.2 2.4 copy.66
  307.7 6.1 %multiply_convert_fusion = bf16[8,128,512]{2,1,0:T(8,128)(2,1)} fusion(bf16[512,8,512]{2,1,0:T(8,128)(2,1)} %bitcast.116, f32[8,512,128]{2,1,0:T(8,128)S(1)} %copy-done.6), kind=kOutput, calls=%fused_computation.32 | convolution fusion | flops 542638080 | bytes 7340032 | tf_op jit(solution)/shard_map/rjm,rjc->mjc/dot_general | solution.py:94
  313.9 2.4 copy.69
  316.5 4.5 fusion.51
  321.1 10.5 %copy.63 = f32[512,8,4,128]{3,1,2,0:T(8,128)} copy(f32[512,8,4,128]{0,3,2,1:T(8,128)} %bitcast.103) | data formatting | bytes 16777216 | tf_op jit(solution)/shard_map/reshape | solution.py:54
  331.5 5.6 %bitcast_convert_fusion = bf16[16,512,128]{2,0,1:T(8,128)(2,1)S(1)} fusion(f32[512,8,4,128]{3,1,2,0:T(8,128)} %copy.63, s32[8,4]{0,1:T(4,128)S(1)} %copy-done.12), kind=kOutput, calls=%fused_computation | convolution fusion | flops 403702272 | bytes 10485888 | tf_op jit(solution)/shard_map/rjkc,jkd->rdc/dot_general | solution.py:55
  339.1 52.5 %reduce-scatter.9.cloned.1.call-done = bf16[16,1024]{1,0:T(8,128)(2,1)} async-done(((bf16[512,1024]{1,0:T(8,128)(2,1)}), bf16[16,1024]{1,0:T(8,128)(2,1)}) %reduce-scatter.9.cloned.1.call-update) | async-done | bytes 32784 | tf_op jit(solution)/shard_map/reduce_scatter | solution.py:102
  393.0 87.2 %reduce-scatter.11.cloned.1.call-done = bf16[16,1024]{1,0:T(8,128)(2,1)} async-done(((bf16[512,1024]{1,0:T(8,128)(2,1)}), bf16[16,1024]{1,0:T(8,128)(2,1)}) %reduce-scatter.11.cloned.1.call-update) | async-done | bytes 32784 | tf_op jit(solution)/shard_map/reduce_scatter | solution.py:99
  481.5 43.7 %reduce-scatter.7.cloned.1.call-done = bf16[64,2048]{1,0:T(8,128)(2,1)} async-done(((bf16[512,2048]{1,0:T(8,128)(2,1)}), bf16[64,2048]{1,0:T(8,128)(2,1)}) %reduce-scatter.7.cloned.1.call-update) | async-done | bytes 262160 | tf_op jit(solution)/shard_map/reduce_scatter | solution.py:106
  526.4 2.0 fusion.35
  (72 shorter events, 23.6 us)
Async XLA Ops:
  7.2 56.7 %all-gather.6.cloned.1.call-start = ((), (), s32[]{:S(2)}) async-start(), calls=%async_computation.6 | async-start | bytes 1081344 | tf_op jit(solution)/shard_map/all_gather | solution.py:34
  7.9 99.0 %all-gather.4.cloned.1.call-start = ((), (), s32[]{:S(2)}) async-start(), calls=%async_computation.5 | async-start | bytes 2359296 | tf_op jit(solution)/shard_map/all_gather | solution.py:42
  10.9 166.2 %reduce-scatter.5.cloned.1.call-start = ((), (), s32[]{:S(2)}) async-start(), calls=%async_computation.7 | async-start | bytes 2359296 | tf_op jit(solution)/shard_map/reduce_scatter | solution.py:64
  106.9 2.2 copy-start.12
  111.1 1.9 copy-start.1
  113.0 4.6 copy-start.4
  135.5 0.7 copy-start.16
  135.5 41.6 %copy-start = (bf16[64,2048]{1,0:T(8,128)(2,1)S(1)}, bf16[64,2048]{1,0:T(8,128)(2,1)}, u32[]{:S(2)}) copy-start(bf16[64,2048]{1,0:T(8,128)(2,1)} %param.9) | copy-start | bytes 786436
  135.5 43.3 %copy-start.14 = (f32[2048]{0:T(1024)S(1)}, f32[2048]{0:T(1024)}, u32[]{:S(2)}) copy-start(f32[2048]{0:T(1024)} %param.17) | copy-start | bytes 24580
  135.5 118.4 %copy-start.15 = (f32[1024]{0:T(1024)S(1)}, f32[1024]{0:T(1024)}, u32[]{:S(2)}) copy-start(f32[1024]{0:T(1024)} %param.15) | copy-start | bytes 12292
  135.5 118.6 %copy-start.9 = (bf16[64,2048]{1,0:T(8,128)(2,1)S(1)}, bf16[64,2048]{1,0:T(8,128)(2,1)}, u32[]{:S(2)}) copy-start(bf16[64,2048]{1,0:T(8,128)(2,1)} %param.16) | copy-start | bytes 786436
  135.5 157.1 %all-gather.8.cloned.1.call-start = ((), (), s32[]{:S(2)}) async-start(), calls=%async_computation.8 | async-start | bytes 2359296 | tf_op jit(solution)/shard_map/all_gather | solution.py:81
  178.1 0.7 copy-start.11
  255.0 136.6 %reduce-scatter.9.cloned.1.call-start = ((), (), s32[]{:S(2)}) async-start(), calls=%async_computation.10 | async-start | bytes 1081344 | tf_op jit(solution)/shard_map/reduce_scatter | solution.py:102
  296.2 1.6 copy-start.5
  296.9 4.7 copy-start.3
  297.8 3.8 copy-start.2
  301.6 3.6 copy-start.7
  305.2 2.5 copy-start.6
  307.7 172.4 %reduce-scatter.11.cloned.1.call-start = ((), (), s32[]{:S(2)}) async-start(), calls=%async_computation.11 | async-start | bytes 1081344 | tf_op jit(solution)/shard_map/reduce_scatter | solution.py:99
  313.9 2.6 copy-start.8
  316.3 209.0 %reduce-scatter.7.cloned.1.call-start = ((), (), s32[]{:S(2)}) async-start(), calls=%async_computation.9 | async-start | bytes 2359296 | tf_op jit(solution)/shard_map/reduce_scatter | solution.py:106
  339.0 186.2 %copy-start.13 = (f32[2048]{0:T(1024)S(1)}, f32[2048]{0:T(1024)}, u32[]{:S(2)}) copy-start(f32[2048]{0:T(1024)} %param.10) | copy-start | bytes 24580
  339.0 187.4 %copy-start.10 = (bf16[64,2048]{1,0:T(8,128)(2,1)S(1)}, bf16[64,2048]{1,0:T(8,128)(2,1)}, u32[]{:S(2)}) copy-start(bf16[64,2048]{1,0:T(8,128)(2,1)} %param.16) | copy-start | bytes 786436
Sparse Core Ops, SparseCore 0:
  10.5 53.2 all-gather.5
  66.2 40.5 all-gather.3
  135.7 41.3 reduce-scatter.4
  255.1 37.5 all-gather.7
  307.8 83.7 reduce-scatter.8
  395.2 84.8 reduce-scatter.10
  482.7 42.5 reduce-scatter.6
